TPU v7x, 256 devices: a whole 4x4x8 slice. The times are simulated.
256 devices in a mesh: frame: 16 (over y, z_hi, core), row: 16 (over x, z_lo).
Axes of the slice: x: 4, y: 4, z: 8 (z_hi: 2, z_lo: 4; z = z_hi * 4 + z_lo), core: 2. Of those that a mesh axis runs over, the one named last changes fastest.
Arguments:
- spatial_q: bfloat16 [32, 128, 32, 1152], P('frame', 'row'), may hold values from -10.5 to 10.5
- spatial_k: bfloat16 [32, 128, 32, 1152], P('frame', 'row'), may hold values from -10.5 to 10.5
- spatial_v: bfloat16 [32, 128, 32, 1152], P('frame', 'row'), may hold values from -6 to 6
- residual: bfloat16 [32, 128, 32, 1152], P('frame', 'row'), may hold values from -6 to 6
- neighbour_list: int32 [64, 6], P('row'), may hold values from 0 to 15, as said below
- block_mask: int32 [8, 8], replicated, may hold values from 0 to 1, as said below
- out_weight: bfloat16 [1152, 1152], P('frame'), may hold values from -0.1875 to 0.1875
- qkv_weight: bfloat16 [1152, 3456], P('frame'), may hold values from -1.4799 to 1.4799
- pos_embed: float32 [32, 1152], P('frame'), may hold values from -150.5 to 150.5
- mod_shift: float32 [1152], replicated, may hold values from -2 to 2
- mod_scale: float32 [1152], replicated, may hold values from -2 to 2
Outputs:
- temporal_mix: bfloat16 [32, 128, 32, 1152], P('frame', 'row')
Inputs may be any that keep to these rules, and one draw needn't show every extreme that they name: `neighbour_list`: each row holds 6 different tiles of its own clip: slot 0 is the row's own tile; every other lies at most one tile row and at most two tile columns away from it, inside the grid of 16 tiles. `block_mask`: entry (i, j) is 1 where i == j and 0 where j > i.
All inputs are finite; a program needn't handle non-finite values.
Results may differ from a plain program's by a relative error of at most 0.0056.
The roundings to bfloat16 on the way count: a program that leaves them out, or rounds other values in their place, can miss the bound.
Values may be sent and summed in bfloat16 or wider, within the bound.
No kernel may reach another device: no remote copies, remote signals or barrier semaphores. Data moves between devices by JAX's collectives and lax.ppermute only.
A program may use at most 128 MiB of HBM per device.

v0:
```python
import math
import jax
import jax.numpy as jnp
from jax import lax
from jax.sharding import PartitionSpec as P

HEADS = 16
TILE = 8
SLOTS = 6
ROWS = 32
BLOCK = 4
EPS = 1e-06
ROW_AXIS = ("x", "zl")
FRAME_AXIS = ("y", "zh", "core")


def padded(block):
    count = lax.axis_size(ROW_AXIS)
    down = [(i, (i + 1) % count) for i in range(count) if (i + 1) % 4 != 3]
    up = [(target, source) for source, target in down]
    low = lax.ppermute(block, ROW_AXIS, down)
    high = lax.ppermute(block, ROW_AXIS, up)
    return jnp.concatenate([low, block, high], axis=2)


def gathered(weight):
    other = lax.ppermute(weight, ("zh", "zl"), [(i, 7 - i) for i in range(8)])
    first = lax.axis_index("zh") == 0
    pair = jnp.stack((jnp.where(first, weight, other), jnp.where(first, other, weight)), 0)
    full = lax.all_gather(pair, ("y", "core"), axis=0, tiled=False)
    rows, cols = weight.shape
    full = full.reshape(4, 2, 2, rows, cols)
    return jnp.transpose(full, (0, 2, 1, 3, 4)).reshape(16 * rows, cols)


def tiles_of(field):
    leading = field.shape[:-3]
    height, breadth, channels = field.shape[-3:]
    tile_grid = field.reshape(leading + (height // TILE, TILE, breadth // TILE, TILE, channels))
    lead_count = len(leading)
    arrangement = tuple(range(lead_count)) + (
        lead_count,
        lead_count + 2,
        lead_count + 1,
        lead_count + 3,
        lead_count + 4,
    )
    tile_grid = jnp.transpose(tile_grid, arrangement)
    return tile_grid.reshape(leading + (height // TILE * (breadth // TILE), TILE * TILE, channels))


def untile(tiles, height, breadth):
    leading = tiles.shape[:-3]
    channels = tiles.shape[-1]
    tile_grid = tiles.reshape(leading + (height // TILE, breadth // TILE, TILE, TILE, channels))
    lead_count = len(leading)
    arrangement = tuple(range(lead_count)) + (
        lead_count,
        lead_count + 2,
        lead_count + 1,
        lead_count + 3,
        lead_count + 4,
    )
    return jnp.transpose(tile_grid, arrangement).reshape(leading + (height, breadth, channels))


def window_attention(queries, keys, values):
    tile_count, token_count, channels = queries.shape
    head_size = channels // HEADS
    shaped_q = queries.reshape(tile_count, token_count, HEADS, head_size)
    shaped_k = keys.reshape(tile_count, -1, HEADS, head_size)
    shaped_v = values.reshape(tile_count, -1, HEADS, head_size)
    scores = jnp.einsum(
        "tqhe,tkhe->thqk", shaped_q, shaped_k, preferred_element_type=jnp.float32
    ) * (1.0 / math.sqrt(head_size))
    peak = jnp.max(scores, axis=-1, keepdims=True)
    powers = jnp.exp(scores - peak)
    weights = (powers / jnp.sum(powers, axis=-1, keepdims=True)).astype(jnp.bfloat16)
    mixed = jnp.einsum("thqk,tkhe->tqhe", weights, shaped_v, preferred_element_type=jnp.float32)
    return mixed.astype(jnp.bfloat16).reshape(tile_count, token_count, channels)


def frame_attention(queries, keys, values, allowed):
    frame_count, spot_count, channels = queries.shape
    head_size = channels // HEADS
    shaped_q = queries.reshape(frame_count, spot_count, HEADS, head_size)
    shaped_k = keys.reshape(frame_count, spot_count, HEADS, head_size)
    shaped_v = values.reshape(frame_count, spot_count, HEADS, head_size)
    scores = jnp.einsum(
        "fphe,gphe->phfg", shaped_q, shaped_k, preferred_element_type=jnp.float32
    ) * (1.0 / math.sqrt(head_size))
    scores = jnp.where(allowed, scores, -jnp.inf)
    peak = jnp.max(scores, axis=-1, keepdims=True)
    powers = jnp.exp(scores - peak)
    weights = (powers / jnp.sum(powers, axis=-1, keepdims=True)).astype(jnp.bfloat16)
    mixed = jnp.einsum("phfg,gphe->fphe", weights, shaped_v, preferred_element_type=jnp.float32)
    return mixed.astype(jnp.bfloat16).reshape(frame_count, spot_count, channels)


def normalize(field, mod_shift, mod_scale):
    average = jnp.mean(field, axis=-1, keepdims=True)
    centred = field - average
    spread = jnp.mean(centred * centred, axis=-1, keepdims=True)
    return centred * lax.rsqrt(spread + EPS) * (1.0 + mod_scale) + mod_shift


def fold_with(left, piece):
    return jnp.dot(left, piece, preferred_element_type=jnp.float32)


def frame_window(items):
    return window_attention(items[0], items[1], items[2])


def local(
    spatial_q,
    spatial_k,
    spatial_v,
    residual,
    neighbour_list,
    block_mask,
    out_weight,
    qkv_weight,
    pos_embed,
    mod_shift,
    mod_scale,
):
    frames_here, height, breadth, channels = spatial_q.shape
    tiles_wide = breadth // TILE
    tokens_here = frames_here * height * breadth
    stacked = jnp.stack((spatial_k, spatial_v), 0)
    rims = padded(stacked)
    key_tiles = tiles_of(rims)
    tile_row_here = (lax.axis_index(ROW_AXIS) + 1) % (ROWS // TILE)
    local_ids = (
        (neighbour_list // tiles_wide - tile_row_here + 1) * tiles_wide
        + neighbour_list % tiles_wide
    ).reshape(-1)
    picked = jnp.take(key_tiles, local_ids, axis=2).reshape(
        2, frames_here, tiles_wide, SLOTS * TILE * TILE, channels
    )
    query_tiles = tiles_of(spatial_q)
    attended = lax.map(frame_window, (query_tiles, picked[0], picked[1]))
    heads = untile(attended, height, breadth).reshape(tokens_here, channels)
    spatial_sum = fold_with(heads, gathered(out_weight))
    mixed = (residual.reshape(tokens_here, channels).astype(jnp.float32) + spatial_sum).astype(
        jnp.bfloat16
    )
    mixed = lax.optimization_barrier(mixed)
    shifted = (
        mixed.astype(jnp.float32).reshape(frames_here, height * breadth, channels)
        + pos_embed[:, None, :]
    )
    normed = normalize(shifted, mod_shift, mod_scale).astype(jnp.bfloat16)
    normed = lax.all_to_all(normed, FRAME_AXIS, split_axis=1, concat_axis=0, tiled=True)
    projected = fold_with(normed.reshape(tokens_here, channels), gathered(qkv_weight)).astype(
        jnp.bfloat16
    )
    projected = projected.reshape(-1, tokens_here // 32, 3 * channels)
    allowed = jnp.repeat(jnp.repeat(block_mask, BLOCK, axis=0), BLOCK, axis=1) == 1
    temporal = frame_attention(
        projected[..., :channels],
        projected[..., channels : 2 * channels],
        projected[..., 2 * channels :],
        allowed,
    )
    returned = lax.all_to_all(temporal, FRAME_AXIS, split_axis=0, concat_axis=1, tiled=True)
    return returned.reshape(frames_here, height, breadth, channels)


def solution(mesh):
    fine = jax.sharding.Mesh(mesh.devices.reshape(4, 2, 2, 4, 4), ("y", "zh", "core", "x", "zl"))
    tokens = P(FRAME_AXIS, ROW_AXIS, None, None)
    return jax.shard_map(
        local,
        mesh=fine,
        in_specs=(
            tokens,
            tokens,
            tokens,
            tokens,
            P(ROW_AXIS, None),
            P(),
            P(FRAME_AXIS, None),
            P(FRAME_AXIS, None),
            P(FRAME_AXIS, None),
            P(),
            P(),
        ),
        out_specs=tokens,
        check_vma=False,
    )
```

profile of v0, /device:TPU:39, one launch (start us, length us, event | category | flops | bytes accessed | tf_op | source)
XLA Modules:
  0.0 384.5 jit_solution(1866561831141859404)
XLA Ops:
  6.5 5.6 %collective-permute-start.2 = (bf16[72,1152]{1,0:T(8,128)(2,1)}, bf16[72,1152]{1,0:T(8,128)(2,1)S(1)}, u32[]{:S(2)}, u32[]{:S(2)}) collective-permute-start(bf16[72,1152]{1,0:T(8,128)(2,1)} %param.19), channel_id=1, source_target_pairs={{0,35},{1,34},{2,33},{3,32},{32,3},{33,2},{34,1},{35,0},{4,39},{5,... | collective-permute-start | bytes 497672 | tf_op jit(solution)/shard_map/ppermute | solution.py:27
  12.1 4.2 %collective-permute-done.2 = bf16[72,1152]{1,0:T(8,128)(2,1)S(1)} collective-permute-done((bf16[72,1152]{1,0:T(8,128)(2,1)}, bf16[72,1152]{1,0:T(8,128)(2,1)S(1)}, u32[]{:S(2)}, u32[]{:S(2)}) %collective-permute-start.2) | collective-permute-done | bytes 165920 | tf_op jit(solution)/shard_map/ppermute | solution.py:27
  23.6 5.0 %collective-permute-start.1 = (bf16[2,2,8,32,1152]{4,3,2,1,0:T(8,128)(2,1)}, bf16[2,2,8,32,1152]{4,3,2,1,0:T(8,128)(2,1)}, u32[]{:S(2)}, u32[]{:S(2)}) collective-permute-start(bf16[2,2,8,32,1152]{4,3,2,1,0:T(8,128)(2,1)} %pad_maximum_fusion.1), channel_id=1, source_target_pairs={{1,0},{2,1},{4,3},{5,4},{6,5},{8,7},{9,8},{10,9},{12,11},{13,12},{... | collective-permute-start | bytes 7077896 | tf_op jit(solution)/shard_map/ppermute | solution.py:22
  28.6 3.5 collective-permute-start.3
  34.1 106.8 %collective-permute-done.3 = bf16[72,3456]{1,0:T(8,128)(2,1)S(1)} collective-permute-done((bf16[72,3456]{1,0:T(8,128)(2,1)S(1)}, bf16[72,3456]{1,0:T(8,128)(2,1)S(1)}, u32[]{:S(2)}, u32[]{:S(2)}) %collective-permute-start.3) | collective-permute-done | bytes 497696 | tf_op jit(solution)/shard_map/ppermute | solution.py:27
  145.5 4.0 %copy.95 = bf16[2,2,3,4,8,8,1152]{6,5,4,3,2,1,0:T(8,128)(2,1)} copy(bf16[2,2,3,4,8,8,1152]{6,5,3,4,2,1,0:T(8,128)(2,1)S(1)} %bitcast.93) | data formatting | bytes 14155776 | tf_op jit(solution)/shard_map/transpose | solution.py:48
  149.5 10.5 %gather_fusion = bf16[24,2,2,64,1152]{4,3,2,1,0:T(8,128)(2,1)} fusion(bf16[2,2,12,64,1152]{4,3,2,1,0:T(8,128)(2,1)} %bitcast.92, s32[1024]{0:T(1024)S(1)} %pad_clamp_fusion), kind=kCustom, calls=%fused_computation | custom fusion | bytes 28311648 | tf_op jit(solution)/shard_map/jit(_take)/gather | solution.py:139
  160.0 7.1 %select_bitcast_fusion = bf16[2,2,24,64,1152]{4,3,1,0,2:T(8,128)(2,1)S(1)} fusion(bf16[24,2,2,64,1152]{4,3,2,1,0:T(8,128)(2,1)} %gather_fusion, pred[24]{0:T(512)(128)(4,1)S(1)} %compare_and_fusion), kind=kLoop, calls=%fused_computation.18 | loop fusion | flops 7077888 | bytes 28311576 | tf_op jit(solution)/shard_map/jit(_take)/select_n | solution.py:139
  168.6 3.6 copy.96
  172.2 3.6 copy.98
  175.8 73.6 %while.10 = (s32[]{:T(128)}, bf16[2,4,64,1152]{3,2,1,0:T(8,128)(2,1)}, bf16[2,4,384,1152]{3,2,1,0:T(8,128)(2,1)}, bf16[2,4,64,1152]{3,2,1,0:T(8,128)(2,1)}, bf16[2,4,384,1152]{3,2,1,0:T(8,128)(2,1)}, /*index=5*/s32[]{:T(128)}) while((s32[]{:T(128)}, bf16[2,4,64,1152]{3,2,1,0:T(8,128)(2,1)}, bf16[2,4,384,1152]{3,2,1,0:T(8,128)(2,1)}, ...), condition=%wide.region_3.4_spmd, body=%wide.region_0.3_spmd.sunk | while | flops 462717312 | bytes 77103232 | solution.py:143
  175.8 5.6 %constant_dynamic-slice_fusion.5 = (bf16[1,4,384,1152]{3,2,1,0:T(8,128)(2,1)}, bf16[1,4,384,1152]{3,2,1,0:T(8,128)(2,1)S(1)}) fusion(bf16[2,4,384,1152]{3,2,1,0:T(8,128)(2,1)} %get-tuple-element.138, s32[]{:T(128)} %get-tuple-element.128, bf16[2,4,384,1152]{3,2,1,0:T(8,128)(2,1)} %get-tuple-element.136), kind=kLoop, calls=%fused_computation.13.clone.1 | loop fusion | bytes 14155780 | tf_op jit(solution)/shard_map/while/body/jit(dynamic_index_in_dim)/dynamic_slice | solution.py:143
  181.5 5.8 %copy.134 = bf16[1,4,384,1152]{2,3,1,0:T(8,128)(2,1)} copy(bf16[1,4,384,1152]{3,2,1,0:T(8,128)(2,1)} %get-tuple-element.119) | data formatting | bytes 7077888 | tf_op jit(solution)/shard_map/while/body/jit(dynamic_index_in_dim)/dynamic_slice | solution.py:143
  189.2 3.7 reshape.191
  196.2 4.6 %fusion.56 = (f32[4,16,64]{2,1,0:T(8,128)}, f32[4,16,64,384]{3,2,1,0:T(8,128)}) fusion(f32[4,16,64,384]{3,2,1,0:T(8,128)S(1)} %fusion.55), kind=kOutput, calls=%fused_computation.72.clone.1 | output fusion | flops 6291839 | bytes 12599296 | tf_op jit(solution)/shard_map/while/body/eval_jaxpr/sub | solution.py:77
  200.8 3.6 copy.133
  204.4 5.3 %fusion.57 = bf16[4,64,16,72]{3,1,2,0:T(8,128)(2,1)S(1)} fusion(bf16[4,384,16,72]{1,3,2,0:T(8,128)(2,1)} %bitcast.89, f32[4,16,64,384]{3,2,1,0:T(8,128)} %get-tuple-element.120, f32[4,16,64]{2,1,0:T(8,128)} %get-tuple-element.121), kind=kOutput, calls=%fused_computation.9.clone.1 | convolution fusion | flops 229933056 | bytes 10436608 | tf_op jit(solution)/shard_map/while/body/eval_jaxpr/thqk,tkhe->tqhe/dot_general | solution.py:79
  212.7 5.5 %constant_dynamic-slice_fusion.5 = (bf16[1,4,384,1152]{3,2,1,0:T(8,128)(2,1)}, bf16[1,4,384,1152]{3,2,1,0:T(8,128)(2,1)S(1)}) fusion(bf16[2,4,384,1152]{3,2,1,0:T(8,128)(2,1)} %get-tuple-element.138, s32[]{:T(128)} %get-tuple-element.128, bf16[2,4,384,1152]{3,2,1,0:T(8,128)(2,1)} %get-tuple-element.136), kind=kLoop, calls=%fused_computation.13.clone.1 | loop fusion | bytes 14155780 | tf_op jit(solution)/shard_map/while/body/jit(dynamic_index_in_dim)/dynamic_slice | solution.py:143
  218.2 5.8 %copy.134 = bf16[1,4,384,1152]{2,3,1,0:T(8,128)(2,1)} copy(bf16[1,4,384,1152]{3,2,1,0:T(8,128)(2,1)} %get-tuple-element.119) | data formatting | bytes 7077888 | tf_op jit(solution)/shard_map/while/body/jit(dynamic_index_in_dim)/dynamic_slice | solution.py:143
  225.9 3.7 reshape.191
  232.9 4.6 %fusion.56 = (f32[4,16,64]{2,1,0:T(8,128)}, f32[4,16,64,384]{3,2,1,0:T(8,128)}) fusion(f32[4,16,64,384]{3,2,1,0:T(8,128)S(1)} %fusion.55), kind=kOutput, calls=%fused_computation.72.clone.1 | output fusion | flops 6291839 | bytes 12599296 | tf_op jit(solution)/shard_map/while/body/eval_jaxpr/sub | solution.py:77
  237.5 3.6 copy.133
  241.1 5.3 %fusion.57 = bf16[4,64,16,72]{3,1,2,0:T(8,128)(2,1)S(1)} fusion(bf16[4,384,16,72]{1,3,2,0:T(8,128)(2,1)} %bitcast.89, f32[4,16,64,384]{3,2,1,0:T(8,128)} %get-tuple-element.120, f32[4,16,64]{2,1,0:T(8,128)} %get-tuple-element.121), kind=kOutput, calls=%fused_computation.9.clone.1 | convolution fusion | flops 229933056 | bytes 10436608 | tf_op jit(solution)/shard_map/while/body/eval_jaxpr/thqk,tkhe->tqhe/dot_general | solution.py:79
  258.5 8.2 %all-to-all-start = ((bf16[2,256,1152]{2,0,1:T(2,128)(2,1)}), bf16[2,256,1152]{2,0,1:T(2,128)(2,1)S(1)}, u32[]{:S(2)}, u32[]{:S(2)}) async-start(bf16[2,256,1152]{2,0,1:T(2,128)(2,1)} %copy.103), calls=%async_computation | async-start | bytes 2359296 | tf_op jit(solution)/shard_map/all_to_all | solution.py:155
  266.8 33.2 %all-to-all-done = bf16[2,256,1152]{2,0,1:T(2,128)(2,1)S(1)} async-done(((bf16[2,256,1152]{2,0,1:T(2,128)(2,1)}), bf16[2,256,1152]{2,0,1:T(2,128)(2,1)S(1)}, u32[]{:S(2)}, u32[]{:S(2)}) %all-to-all-start) | async-done | bytes 1179680 | tf_op jit(solution)/shard_map/all_to_all | solution.py:155
  301.2 3.8 copy.106
  305.0 6.5 %convolution_convert_fusion = bf16[512,3456]{1,0:T(8,128)(2,1)S(1)} fusion(bf16[512,1152]{1,0:T(8,128)(2,1)} %bitcast.108, bf16[1152,3456]{1,0:T(8,128)(2,1)S(1)} %bitcast.96), kind=kOutput, calls=%fused_computation.20 | convolution fusion | flops 4078632960 | bytes 12681216 | tf_op jit(solution)/shard_map/dot_general | solution.py:108
  313.2 5.0 %reshape.173 = bf16[32,16,16,72]{3,2,1,0:T(8,128)(2,1)S(1)} reshape(bf16[32,16,1152]{2,1,0:T(8,128)(2,1)} %get-tuple-element.76) | data formatting | bytes 2359296 | tf_op jit(solution)/shard_map/reshape | solution.py:86
  318.2 5.7 %reshape.174 = bf16[32,16,16,72]{3,2,1,0:T(8,128)(2,1)} reshape(bf16[32,16,1152]{2,1,0:T(8,128)(2,1)} %get-tuple-element.75) | data formatting | bytes 2359296 | tf_op jit(solution)/shard_map/reshape | solution.py:87
  323.9 4.7 %reshape.172 = bf16[32,16,16,72]{3,2,1,0:T(8,128)(2,1)} reshape(bf16[32,16,1152]{2,1,0:T(8,128)(2,1)S(1)} %get-tuple-element.74) | data formatting | bytes 2359296 | tf_op jit(solution)/shard_map/reshape | solution.py:88
  328.6 4.3 %fusion.17 = f32[16,16,32,32]{2,3,1,0:T(8,128)S(1)} fusion(bf16[32,16,16,72]{3,2,1,0:T(8,128)(2,1)} %reshape.174, bf16[32,16,16,72]{3,2,1,0:T(8,128)(2,1)S(1)} %reshape.173), kind=kOutput, calls=%fused_computation.34 | convolution fusion | flops 37748736 | bytes 3407872 | tf_op jit(solution)/shard_map/fphe,gphe->phfg/dot_general | solution.py:89
  340.6 36.0 %all_to_all.30 = bf16[32,16,1152]{2,1,0:T(8,128)(2,1)S(1)} all-to-all(bf16[32,16,1152]{2,1,0:T(8,128)(2,1)} %reshape.175), channel_id=1, replica_groups=mesh['y'=4,'zh'=2,'core'=2,'x'=4,'zl'=4] {'y','zh','core'}, dimensions={0} | all-to-all | bytes 2359296 | tf_op jit(solution)/shard_map/all_to_all | solution.py:167
  (92 shorter events, 52.7 us)
Async XLA Ops:
  6.5 26.4 %copy-start = (bf16[2,8,32,1152]{3,2,1,0:T(8,128)(2,1)S(1)}, bf16[2,8,32,1152]{3,2,1,0:T(8,128)(2,1)}, u32[]{:S(2)}) copy-start(bf16[2,8,32,1152]{3,2,1,0:T(8,128)(2,1)} %param.13) | copy-start | bytes 3538948
  6.5 11.6 %copy-start.2 = (bf16[2,8,32,1152]{3,2,1,0:T(8,128)(2,1)S(1)}, bf16[2,8,32,1152]{3,2,1,0:T(8,128)(2,1)}, u32[]{:S(2)}) copy-start(bf16[2,8,32,1152]{3,2,1,0:T(8,128)(2,1)} %param.15) | copy-start | bytes 3538948
  6.5 244.3 %all-gather.5.cloned.1.call-start = ((), (), s32[]{:S(2)}) async-start(), calls=%async_computation.2 | async-start | bytes 2985984 | tf_op jit(solution)/shard_map/all_gather | solution.py:30
  6.5 9.8 %collective-permute-start.2 = (bf16[72,1152]{1,0:T(8,128)(2,1)}, bf16[72,1152]{1,0:T(8,128)(2,1)S(1)}, u32[]{:S(2)}, u32[]{:S(2)}) collective-permute-start(bf16[72,1152]{1,0:T(8,128)(2,1)} %param.19), channel_id=1, source_target_pairs={{0,35},{1,34},{2,33},{3,32},{32,3},{33,2},{34,1},{35,0},{4,39},{5,... | collective-permute-start | bytes 497672 | tf_op jit(solution)/shard_map/ppermute | solution.py:27
  18.1 283.1 %all-gather.7.cloned.1.call-start = ((), (), s32[]{:S(2)}) async-start(), calls=%async_computation.3 | async-start | bytes 8957952 | tf_op jit(solution)/shard_map/all_gather | solution.py:30
  18.1 10.5 %copy-start.7 = (bf16[72,3456]{1,0:T(8,128)(2,1)S(1)}, bf16[72,3456]{1,0:T(8,128)(2,1)}, u32[]{:S(2)}) copy-start(bf16[72,3456]{1,0:T(8,128)(2,1)} %param.20) | copy-start | bytes 1492996
  18.1 14.0 %copy-start.13 = (s32[4,6]{1,0:T(4,128)S(1)}, s32[4,6]{1,0:T(4,128)}, u32[]{:S(2)}) copy-start(s32[4,6]{1,0:T(4,128)} %param.17) | copy-start | bytes 292
  18.1 14.2 %copy-start.11 = (f32[1152]{0:T(1024)S(1)}, f32[1152]{0:T(1024)}, u32[]{:S(2)}) copy-start(f32[1152]{0:T(1024)} %param.23) | copy-start | bytes 13828
  21.1 120.9 %collective-permute-start = (bf16[2,2,8,32,1152]{4,3,2,1,0:T(8,128)(2,1)}, bf16[2,2,8,32,1152]{4,3,2,1,0:T(8,128)(2,1)}, u32[]{:S(2)}, u32[]{:S(2)}) collective-permute-start(bf16[2,2,8,32,1152]{4,3,2,1,0:T(8,128)(2,1)} %pad_maximum_fusion.1), channel_id=1, source_target_pairs={{0,1},{1,2},{3,4},{4,5},{5,6},{7,8},{8,9},{9,10},{11,12},{12,13},{... | collective-permute-start | bytes 7077896 | tf_op jit(solution)/shard_map/ppermute | solution.py:21
  23.6 118.4 %collective-permute-start.1 = (bf16[2,2,8,32,1152]{4,3,2,1,0:T(8,128)(2,1)}, bf16[2,2,8,32,1152]{4,3,2,1,0:T(8,128)(2,1)}, u32[]{:S(2)}, u32[]{:S(2)}) collective-permute-start(bf16[2,2,8,32,1152]{4,3,2,1,0:T(8,128)(2,1)} %pad_maximum_fusion.1), channel_id=1, source_target_pairs={{1,0},{2,1},{4,3},{5,4},{6,5},{8,7},{9,8},{10,9},{12,11},{13,12},{... | collective-permute-start | bytes 7077896 | tf_op jit(solution)/shard_map/ppermute | solution.py:22
  28.6 112.3 %collective-permute-start.3 = (bf16[72,3456]{1,0:T(8,128)(2,1)S(1)}, bf16[72,3456]{1,0:T(8,128)(2,1)S(1)}, u32[]{:S(2)}, u32[]{:S(2)}) collective-permute-start(bf16[72,3456]{1,0:T(8,128)(2,1)S(1)} %copy-done.7), channel_id=1, source_target_pairs={{0,35},{1,34},{2,33},{3,32},{32,3},{33,2},{34,1},{35,0},{4,39},{5,... | collective-permute-start | bytes 1493000 | tf_op jit(solution)/shard_map/ppermute | solution.py:27
  34.1 108.0 %copy-start.3 = (bf16[2,8,32,1152]{3,2,1,0:T(8,128)(2,1)S(1)}, bf16[2,8,32,1152]{3,2,1,0:T(8,128)(2,1)}, u32[]{:S(2)}) copy-start(bf16[2,8,32,1152]{3,2,1,0:T(8,128)(2,1)} %param.14) | copy-start | bytes 3538948
  209.7 2.0 copy-start.5
  211.7 1.0 copy-start.6
  246.4 2.0 copy-start.5
  248.4 1.0 copy-start.6
  250.9 2.1 copy-start.14
  253.0 1.9 copy-start.8
  254.8 0.9 copy-start.9
  254.8 0.9 copy-start.10
  256.2 10.4 %copy-start.12 = (s32[8,8]{1,0:T(8,128)S(1)}, s32[8,8]{1,0:T(8,128)}, u32[]{:S(2)}) copy-start(s32[8,8]{1,0:T(8,128)} %param.18) | copy-start | bytes 772
  258.5 41.5 %all-to-all-start = ((bf16[2,256,1152]{2,0,1:T(2,128)(2,1)}), bf16[2,256,1152]{2,0,1:T(2,128)(2,1)S(1)}, u32[]{:S(2)}, u32[]{:S(2)}) async-start(bf16[2,256,1152]{2,0,1:T(2,128)(2,1)} %copy.103), calls=%async_computation | async-start | bytes 2359296 | tf_op jit(solution)/shard_map/all_to_all | solution.py:155
  332.9 1.6 copy-start.4
  337.1 40.5 %copy-start.1 = (bf16[2,8,32,1152]{3,2,1,0:T(8,128)(2,1)S(1)}, bf16[2,8,32,1152]{3,2,1,0:T(8,128)(2,1)}, u32[]{:S(2)}) copy-start(bf16[2,8,32,1152]{3,2,1,0:T(8,128)(2,1)} %param.13) | copy-start | bytes 3538948
Sparse Core Ops, SparseCore 0:
  18.2 32.6 all-gather.4
  142.2 52.1 all-gather.6
where the time goes:
time: 386 us; the launch traced here: 385 us
  waiting for transfers between devices  144 us (37%)
  local copies, waits for them, and re-layouts  105 us (27%)
  blocking collectives  36 us (9%)
  matrix products  31.6 us (8%)
  other arithmetic  29 us (8%)
  starting transfers between devices  24.7 us (6%)
  between operations  13.7 us (4%)
    ppermute x2, waiting for transfers between devices, gathered(): other = lax.ppermute(weight, ('zh', 'zl'), [(i, 7 - i) for i in range(8)])  111 us
    all_to_all x1, blocking collectives, local(): lax.all_to_all(temporal, FRAME_AXIS, split_axis=0, concat_axis=1, tiled=T...  36 us
    dynamic_slice x8, local copies, waits for them, and re-layouts, local(): attended = lax.map(frame_window, (query_tiles, picked[0], picked[1]))  33.7 us
    all_to_all x1, waiting for transfers between devices, local(): lax.all_to_all(normed, FRAME_AXIS, split_axis=1, concat_axis=0, tiled=True)  33.2 us
    dot_general x2, matrix products, window_attention(): jnp.einsum('thqk,tkhe->tqhe', weights, shaped_v, preferred_element_type=j...  10.5 us
    gather x1, local copies, waits for them, and re-layouts, local(): jnp.take(key_tiles, local_ids, axis=2)  10.5 us
    sub x2, other arithmetic, window_attention(): powers = jnp.exp(scores - peak)  9.13 us
    ppermute x2, starting transfers between devices, gathered(): other = lax.ppermute(weight, ('zh', 'zl'), [(i, 7 - i) for i in range(8)])  9.05 us
  transfers between devices with their start and end apart: 7, of which 3 were waited for; matrix products, arithmetic and copies ran while one was open for 32% of the time, Pallas kernels for 0%

commit v1 on v0

--- a/solution.py
+++ b/solution.py
@@ -164,7 +164,12 @@
         projected[..., 2 * channels :],
         allowed,
     )
-    returned = lax.all_to_all(temporal, FRAME_AXIS, split_axis=0, concat_axis=1, tiled=True)
+    returned = jnp.concatenate(
+        lax.all_to_all(
+            jnp.stack(jnp.split(temporal, lax.axis_size(FRAME_AXIS), axis=0)), FRAME_AXIS, 0, 0
+        ),
+        axis=1,
+    )
     return returned.reshape(frames_here, height, breadth, channels)
 
 

time: 386 us -> 393 us (1.018); the launches traced: 385 us -> 387 us
  transfers between devices with their start and end apart: 7 -> 7, of which waited for: 3 -> 3; matrix products, arithmetic and copies ran while one was open for 32% -> 31% of each run, Pallas kernels for 0% -> 0%
where the time goes in v1:
time: 393 us; the launch traced here: 387 us
  waiting for transfers between devices  144 us (37%)
  local copies, waits for them, and re-layouts  107 us (27%)
  blocking collectives  35.9 us (9%)
  matrix products  31.6 us (8%)
  other arithmetic  29 us (7%)
  starting transfers between devices  24.6 us (6%)
  between operations  14.1 us (4%)
    ppermute x2, waiting for transfers between devices, gathered(): other = lax.ppermute(weight, ('zh', 'zl'), [(i, 7 - i) for i in range(8)])  111 us
    all_to_all x1, blocking collectives, local(): lax.all_to_all(jnp.stack(jnp.split(temporal, lax.axis_size(FRAME_AXIS), a...  35.9 us
    dynamic_slice x8, local copies, waits for them, and re-layouts, local(): attended = lax.map(frame_window, (query_tiles, picked[0], picked[1]))  33.8 us
    all_to_all x1, waiting for transfers between devices, local(): lax.all_to_all(normed, FRAME_AXIS, split_axis=1, concat_axis=0, tiled=True)  33.3 us
    dot_general x2, matrix products, window_attention(): jnp.einsum('thqk,tkhe->tqhe', weights, shaped_v, preferred_element_type=j...  10.5 us
    gather x1, local copies, waits for them, and re-layouts, local(): jnp.take(key_tiles, local_ids, axis=2)  10.5 us
    sub x2, other arithmetic, window_attention(): powers = jnp.exp(scores - peak)  9.15 us
    ppermute x2, starting transfers between devices, gathered(): other = lax.ppermute(weight, ('zh', 'zl'), [(i, 7 - i) for i in range(8)])  9.05 us
  transfers between devices with their start and end apart: 7, of which 3 were waited for; matrix products, arithmetic and copies ran while one was open for 31% of the time, Pallas kernels for 0%

profile of v1, /device:TPU:39, one launch (start us, length us, event | category | flops | bytes accessed | tf_op | source)
XLA Modules:
  0.0 387.0 jit_solution(1370045368260239863)
XLA Ops:
  6.5 5.6 %collective-permute-start.2 = (bf16[72,1152]{1,0:T(8,128)(2,1)}, bf16[72,1152]{1,0:T(8,128)(2,1)S(1)}, u32[]{:S(2)}, u32[]{:S(2)}) collective-permute-start(bf16[72,1152]{1,0:T(8,128)(2,1)} %param.19), channel_id=1, source_target_pairs={{0,35},{1,34},{2,33},{3,32},{32,3},{33,2},{34,1},{35,0},{4,39},{5,... | collective-permute-start | bytes 497672 | tf_op jit(solution)/shard_map/ppermute | solution.py:27
  12.1 4.2 %collective-permute-done.2 = bf16[72,1152]{1,0:T(8,128)(2,1)S(1)} collective-permute-done((bf16[72,1152]{1,0:T(8,128)(2,1)}, bf16[72,1152]{1,0:T(8,128)(2,1)S(1)}, u32[]{:S(2)}, u32[]{:S(2)}) %collective-permute-start.2) | collective-permute-done | bytes 165920 | tf_op jit(solution)/shard_map/ppermute | solution.py:27
  23.6 5.0 %collective-permute-start.1 = (bf16[2,2,8,32,1152]{4,3,2,1,0:T(8,128)(2,1)}, bf16[2,2,8,32,1152]{4,3,2,1,0:T(8,128)(2,1)}, u32[]{:S(2)}, u32[]{:S(2)}) collective-permute-start(bf16[2,2,8,32,1152]{4,3,2,1,0:T(8,128)(2,1)} %pad_maximum_fusion.1), channel_id=1, source_target_pairs={{1,0},{2,1},{4,3},{5,4},{6,5},{8,7},{9,8},{10,9},{12,11},{13,12},{... | collective-permute-start | bytes 7077896 | tf_op jit(solution)/shard_map/ppermute | solution.py:22
  28.6 3.5 collective-permute-start.3
  34.1 106.8 %collective-permute-done.3 = bf16[72,3456]{1,0:T(8,128)(2,1)S(1)} collective-permute-done((bf16[72,3456]{1,0:T(8,128)(2,1)S(1)}, bf16[72,3456]{1,0:T(8,128)(2,1)S(1)}, u32[]{:S(2)}, u32[]{:S(2)}) %collective-permute-start.3) | collective-permute-done | bytes 497696 | tf_op jit(solution)/shard_map/ppermute | solution.py:27
  145.5 4.0 %copy.155 = bf16[2,2,3,4,8,8,1152]{6,5,4,3,2,1,0:T(8,128)(2,1)} copy(bf16[2,2,3,4,8,8,1152]{6,5,3,4,2,1,0:T(8,128)(2,1)S(1)} %bitcast.121) | data formatting | bytes 14155776 | tf_op jit(solution)/shard_map/transpose | solution.py:48
  149.5 10.5 %gather_fusion = bf16[24,2,2,64,1152]{4,3,2,1,0:T(8,128)(2,1)} fusion(bf16[2,2,12,64,1152]{4,3,2,1,0:T(8,128)(2,1)} %bitcast.120, s32[1024]{0:T(1024)S(1)} %pad_clamp_fusion), kind=kCustom, calls=%fused_computation | custom fusion | bytes 28311648 | tf_op jit(solution)/shard_map/jit(_take)/gather | solution.py:139
  160.0 7.1 %select_bitcast_fusion = bf16[2,2,24,64,1152]{4,3,1,0,2:T(8,128)(2,1)S(1)} fusion(bf16[24,2,2,64,1152]{4,3,2,1,0:T(8,128)(2,1)} %gather_fusion, pred[24]{0:T(512)(128)(4,1)S(1)} %compare_and_fusion), kind=kLoop, calls=%fused_computation.18 | loop fusion | flops 7077888 | bytes 28311576 | tf_op jit(solution)/shard_map/jit(_take)/select_n | solution.py:139
  168.6 3.6 copy.156
  172.2 3.6 copy.158
  175.8 74.3 %while.10 = (s32[]{:T(128)}, bf16[2,4,64,1152]{3,2,1,0:T(8,128)(2,1)}, bf16[2,4,384,1152]{3,2,1,0:T(8,128)(2,1)}, bf16[2,4,64,1152]{3,2,1,0:T(8,128)(2,1)}, bf16[2,4,384,1152]{3,2,1,0:T(8,128)(2,1)}, /*index=5*/s32[]{:T(128)}) while((s32[]{:T(128)}, bf16[2,4,64,1152]{3,2,1,0:T(8,128)(2,1)}, bf16[2,4,384,1152]{3,2,1,0:T(8,128)(2,1)}, ...), condition=%wide.region_3.4_spmd, body=%wide.region_0.3_spmd.sunk | while | flops 462717312 | bytes 77103232 | solution.py:143
  176.3 5.6 %constant_dynamic-slice_fusion.5 = (bf16[1,4,384,1152]{3,2,1,0:T(8,128)(2,1)}, bf16[1,4,384,1152]{3,2,1,0:T(8,128)(2,1)S(1)}) fusion(bf16[2,4,384,1152]{3,2,1,0:T(8,128)(2,1)} %get-tuple-element.154, s32[]{:T(128)} %get-tuple-element.144, bf16[2,4,384,1152]{3,2,1,0:T(8,128)(2,1)} %get-tuple-element.152), kind=kLoop, calls=%fused_computation.13.clone.1 | loop fusion | bytes 14155780 | tf_op jit(solution)/shard_map/while/body/jit(dynamic_index_in_dim)/dynamic_slice | solution.py:143
  181.9 5.8 %copy.209 = bf16[1,4,384,1152]{2,3,1,0:T(8,128)(2,1)} copy(bf16[1,4,384,1152]{3,2,1,0:T(8,128)(2,1)} %get-tuple-element.135) | data formatting | bytes 7077888 | tf_op jit(solution)/shard_map/while/body/jit(dynamic_index_in_dim)/dynamic_slice | solution.py:143
  189.7 3.7 reshape.219
  196.7 4.6 %fusion.57 = (f32[4,16,64]{2,1,0:T(8,128)}, f32[4,16,64,384]{3,2,1,0:T(8,128)}) fusion(f32[4,16,64,384]{3,2,1,0:T(8,128)S(1)} %fusion.56), kind=kOutput, calls=%fused_computation.88.clone.1 | output fusion | flops 6291839 | bytes 12599296 | tf_op jit(solution)/shard_map/while/body/eval_jaxpr/sub | solution.py:77
  201.3 3.6 copy.208
  204.9 5.3 %fusion.58 = bf16[4,64,16,72]{3,1,2,0:T(8,128)(2,1)S(1)} fusion(bf16[4,384,16,72]{1,3,2,0:T(8,128)(2,1)} %bitcast.117, f32[4,16,64,384]{3,2,1,0:T(8,128)} %get-tuple-element.136, f32[4,16,64]{2,1,0:T(8,128)} %get-tuple-element.137), kind=kOutput, calls=%fused_computation.9.clone.1 | convolution fusion | flops 229933056 | bytes 10436608 | tf_op jit(solution)/shard_map/while/body/eval_jaxpr/thqk,tkhe->tqhe/dot_general | solution.py:79
  213.3 5.5 %constant_dynamic-slice_fusion.5 = (bf16[1,4,384,1152]{3,2,1,0:T(8,128)(2,1)}, bf16[1,4,384,1152]{3,2,1,0:T(8,128)(2,1)S(1)}) fusion(bf16[2,4,384,1152]{3,2,1,0:T(8,128)(2,1)} %get-tuple-element.154, s32[]{:T(128)} %get-tuple-element.144, bf16[2,4,384,1152]{3,2,1,0:T(8,128)(2,1)} %get-tuple-element.152), kind=kLoop, calls=%fused_computation.13.clone.1 | loop fusion | bytes 14155780 | tf_op jit(solution)/shard_map/while/body/jit(dynamic_index_in_dim)/dynamic_slice | solution.py:143
  218.8 5.8 %copy.209 = bf16[1,4,384,1152]{2,3,1,0:T(8,128)(2,1)} copy(bf16[1,4,384,1152]{3,2,1,0:T(8,128)(2,1)} %get-tuple-element.135) | data formatting | bytes 7077888 | tf_op jit(solution)/shard_map/while/body/jit(dynamic_index_in_dim)/dynamic_slice | solution.py:143
  226.5 3.7 reshape.219
  233.5 4.6 %fusion.57 = (f32[4,16,64]{2,1,0:T(8,128)}, f32[4,16,64,384]{3,2,1,0:T(8,128)}) fusion(f32[4,16,64,384]{3,2,1,0:T(8,128)S(1)} %fusion.56), kind=kOutput, calls=%fused_computation.88.clone.1 | output fusion | flops 6291839 | bytes 12599296 | tf_op jit(solution)/shard_map/while/body/eval_jaxpr/sub | solution.py:77
  238.1 3.6 copy.208
  241.7 5.3 %fusion.58 = bf16[4,64,16,72]{3,1,2,0:T(8,128)(2,1)S(1)} fusion(bf16[4,384,16,72]{1,3,2,0:T(8,128)(2,1)} %bitcast.117, f32[4,16,64,384]{3,2,1,0:T(8,128)} %get-tuple-element.136, f32[4,16,64]{2,1,0:T(8,128)} %get-tuple-element.137), kind=kOutput, calls=%fused_computation.9.clone.1 | convolution fusion | flops 229933056 | bytes 10436608 | tf_op jit(solution)/shard_map/while/body/eval_jaxpr/thqk,tkhe->tqhe/dot_general | solution.py:79
  259.2 8.1 %all-to-all-start = ((bf16[2,256,1152]{2,0,1:T(2,128)(2,1)}), bf16[2,256,1152]{2,0,1:T(2,128)(2,1)S(1)}, u32[]{:S(2)}, u32[]{:S(2)}) async-start(bf16[2,256,1152]{2,0,1:T(2,128)(2,1)} %copy.163), calls=%async_computation | async-start | bytes 2359296 | tf_op jit(solution)/shard_map/all_to_all | solution.py:155
  267.4 33.3 %all-to-all-done = bf16[2,256,1152]{2,0,1:T(2,128)(2,1)S(1)} async-done(((bf16[2,256,1152]{2,0,1:T(2,128)(2,1)}), bf16[2,256,1152]{2,0,1:T(2,128)(2,1)S(1)}, u32[]{:S(2)}, u32[]{:S(2)}) %all-to-all-start) | async-done | bytes 1179680 | tf_op jit(solution)/shard_map/all_to_all | solution.py:155
  301.9 3.8 copy.166
  305.7 6.5 %convolution_convert_fusion = bf16[512,3456]{1,0:T(8,128)(2,1)S(1)} fusion(bf16[512,1152]{1,0:T(8,128)(2,1)} %bitcast.136, bf16[1152,3456]{1,0:T(8,128)(2,1)S(1)} %bitcast.124), kind=kOutput, calls=%fused_computation.20 | convolution fusion | flops 4078632960 | bytes 12681216 | tf_op jit(solution)/shard_map/dot_general | solution.py:108
  313.9 5.0 %reshape.202 = bf16[32,16,16,72]{3,2,1,0:T(8,128)(2,1)S(1)} reshape(bf16[32,16,1152]{2,1,0:T(8,128)(2,1)} %get-tuple-element.76) | data formatting | bytes 2359296 | tf_op jit(solution)/shard_map/reshape | solution.py:86
  318.9 5.7 %reshape.203 = bf16[32,16,16,72]{3,2,1,0:T(8,128)(2,1)} reshape(bf16[32,16,1152]{2,1,0:T(8,128)(2,1)} %get-tuple-element.75) | data formatting | bytes 2359296 | tf_op jit(solution)/shard_map/reshape | solution.py:87
  324.6 4.9 %reshape.201 = bf16[32,16,16,72]{3,2,1,0:T(8,128)(2,1)} reshape(bf16[32,16,1152]{2,1,0:T(8,128)(2,1)S(1)} %get-tuple-element.74) | data formatting | bytes 2359296 | tf_op jit(solution)/shard_map/reshape | solution.py:88
  329.5 4.3 %fusion.17 = f32[16,16,32,32]{2,3,1,0:T(8,128)S(1)} fusion(bf16[32,16,16,72]{3,2,1,0:T(8,128)(2,1)} %reshape.203, bf16[32,16,16,72]{3,2,1,0:T(8,128)(2,1)S(1)} %reshape.202), kind=kOutput, calls=%fused_computation.34 | convolution fusion | flops 37748736 | bytes 3407872 | tf_op jit(solution)/shard_map/fphe,gphe->phfg/dot_general | solution.py:89
  342.9 35.9 %all_to_all.20 = bf16[16,2,16,1152]{3,2,1,0:T(8,128)(2,1)S(1)} all-to-all(bf16[16,2,16,1152]{3,2,1,0:T(8,128)(2,1)S(1)} %constant_dynamic-update-slice_fusion.1), channel_id=1, replica_groups=mesh['y'=4,'zh'=2,'core'=2,'x'=4,'zl'=4] {'y','zh','core'}, dimensions={0} | all-to-all | bytes 2359296 | tf_op jit(solution)/shard_map/all_to_all | solution.py:168
  (139 shorter events, 54.0 us)
Async XLA Ops:
  6.5 26.4 %copy-start = (bf16[2,8,32,1152]{3,2,1,0:T(8,128)(2,1)S(1)}, bf16[2,8,32,1152]{3,2,1,0:T(8,128)(2,1)}, u32[]{:S(2)}) copy-start(bf16[2,8,32,1152]{3,2,1,0:T(8,128)(2,1)} %param.13) | copy-start | bytes 3538948
  6.5 11.6 %copy-start.2 = (bf16[2,8,32,1152]{3,2,1,0:T(8,128)(2,1)S(1)}, bf16[2,8,32,1152]{3,2,1,0:T(8,128)(2,1)}, u32[]{:S(2)}) copy-start(bf16[2,8,32,1152]{3,2,1,0:T(8,128)(2,1)} %param.15) | copy-start | bytes 3538948
  6.5 245.1 %all-gather.5.cloned.1.call-start = ((), (), s32[]{:S(2)}) async-start(), calls=%async_computation.2 | async-start | bytes 2985984 | tf_op jit(solution)/shard_map/all_gather | solution.py:30
  6.5 9.8 %collective-permute-start.2 = (bf16[72,1152]{1,0:T(8,128)(2,1)}, bf16[72,1152]{1,0:T(8,128)(2,1)S(1)}, u32[]{:S(2)}, u32[]{:S(2)}) collective-permute-start(bf16[72,1152]{1,0:T(8,128)(2,1)} %param.19), channel_id=1, source_target_pairs={{0,35},{1,34},{2,33},{3,32},{32,3},{33,2},{34,1},{35,0},{4,39},{5,... | collective-permute-start | bytes 497672 | tf_op jit(solution)/shard_map/ppermute | solution.py:27
  18.1 283.9 %all-gather.7.cloned.1.call-start = ((), (), s32[]{:S(2)}) async-start(), calls=%async_computation.3 | async-start | bytes 8957952 | tf_op jit(solution)/shard_map/all_gather | solution.py:30
  18.1 10.5 %copy-start.7 = (bf16[72,3456]{1,0:T(8,128)(2,1)S(1)}, bf16[72,3456]{1,0:T(8,128)(2,1)}, u32[]{:S(2)}) copy-start(bf16[72,3456]{1,0:T(8,128)(2,1)} %param.20) | copy-start | bytes 1492996
  18.1 14.0 %copy-start.13 = (s32[4,6]{1,0:T(4,128)S(1)}, s32[4,6]{1,0:T(4,128)}, u32[]{:S(2)}) copy-start(s32[4,6]{1,0:T(4,128)} %param.17) | copy-start | bytes 292
  18.1 14.2 %copy-start.11 = (f32[1152]{0:T(1024)S(1)}, f32[1152]{0:T(1024)}, u32[]{:S(2)}) copy-start(f32[1152]{0:T(1024)} %param.23) | copy-start | bytes 13828
  21.1 121.0 %collective-permute-start = (bf16[2,2,8,32,1152]{4,3,2,1,0:T(8,128)(2,1)}, bf16[2,2,8,32,1152]{4,3,2,1,0:T(8,128)(2,1)}, u32[]{:S(2)}, u32[]{:S(2)}) collective-permute-start(bf16[2,2,8,32,1152]{4,3,2,1,0:T(8,128)(2,1)} %pad_maximum_fusion.1), channel_id=1, source_target_pairs={{0,1},{1,2},{3,4},{4,5},{5,6},{7,8},{8,9},{9,10},{11,12},{12,13},{... | collective-permute-start | bytes 7077896 | tf_op jit(solution)/shard_map/ppermute | solution.py:21
  23.6 118.4 %collective-permute-start.1 = (bf16[2,2,8,32,1152]{4,3,2,1,0:T(8,128)(2,1)}, bf16[2,2,8,32,1152]{4,3,2,1,0:T(8,128)(2,1)}, u32[]{:S(2)}, u32[]{:S(2)}) collective-permute-start(bf16[2,2,8,32,1152]{4,3,2,1,0:T(8,128)(2,1)} %pad_maximum_fusion.1), channel_id=1, source_target_pairs={{1,0},{2,1},{4,3},{5,4},{6,5},{8,7},{9,8},{10,9},{12,11},{13,12},{... | collective-permute-start | bytes 7077896 | tf_op jit(solution)/shard_map/ppermute | solution.py:22
  28.6 112.3 %collective-permute-start.3 = (bf16[72,3456]{1,0:T(8,128)(2,1)S(1)}, bf16[72,3456]{1,0:T(8,128)(2,1)S(1)}, u32[]{:S(2)}, u32[]{:S(2)}) collective-permute-start(bf16[72,3456]{1,0:T(8,128)(2,1)S(1)} %copy-done.7), channel_id=1, source_target_pairs={{0,35},{1,34},{2,33},{3,32},{32,3},{33,2},{34,1},{35,0},{4,39},{5,... | collective-permute-start | bytes 1493000 | tf_op jit(solution)/shard_map/ppermute | solution.py:27
  34.1 108.0 %copy-start.3 = (bf16[2,8,32,1152]{3,2,1,0:T(8,128)(2,1)S(1)}, bf16[2,8,32,1152]{3,2,1,0:T(8,128)(2,1)}, u32[]{:S(2)}) copy-start(bf16[2,8,32,1152]{3,2,1,0:T(8,128)(2,1)} %param.14) | copy-start | bytes 3538948
  210.2 2.0 copy-start.5
  212.3 1.0 copy-start.6
  247.0 2.0 copy-start.5
  249.0 1.0 copy-start.6
  251.6 2.1 copy-start.14
  253.7 1.9 copy-start.8
  255.5 0.9 copy-start.9
  255.6 0.9 copy-start.10
  257.0 10.3 %copy-start.12 = (s32[8,8]{1,0:T(8,128)S(1)}, s32[8,8]{1,0:T(8,128)}, u32[]{:S(2)}) copy-start(s32[8,8]{1,0:T(8,128)} %param.18) | copy-start | bytes 772
  259.2 41.5 %all-to-all-start = ((bf16[2,256,1152]{2,0,1:T(2,128)(2,1)}), bf16[2,256,1152]{2,0,1:T(2,128)(2,1)S(1)}, u32[]{:S(2)}, u32[]{:S(2)}) async-start(bf16[2,256,1152]{2,0,1:T(2,128)(2,1)} %copy.163), calls=%async_computation | async-start | bytes 2359296 | tf_op jit(solution)/shard_map/all_to_all | solution.py:155
  333.8 1.6 copy-start.4
  342.8 37.1 %copy-start.1 = (bf16[2,8,32,1152]{3,2,1,0:T(8,128)(2,1)S(1)}, bf16[2,8,32,1152]{3,2,1,0:T(8,128)(2,1)}, u32[]{:S(2)}) copy-start(bf16[2,8,32,1152]{3,2,1,0:T(8,128)(2,1)} %param.13) | copy-start | bytes 3538948
Sparse Core Ops, SparseCore 0:
  18.2 32.6 all-gather.4
  142.2 52.1 all-gather.6
